TPU v7x, 32 devices: a whole 2x2x4 slice. The times are simulated.
32 devices in a mesh: batch: 2 (over x), seq: 4 (over y, core), mp: 4 (over z).
Axes of the slice: x: 2, y: 2, z: 4, core: 2. Of those that a mesh axis runs over, the one named last changes fastest.
Arguments:
- context: bfloat16 [1024, 6144], P(('batch', 'seq'), 'mp'), may hold values from -0.25 to 0.25
- cotangent: bfloat16 [1024, 6144], P(('batch', 'seq'), 'mp'), may hold values from -6 to 6
- out_weight: bfloat16 [6144, 6144], P(None, 'mp'), may hold values from -0.078125 to 0.078125
Outputs:
- grad_weight: float32 [6144, 6144], P(('batch', 'seq'), 'mp')
- grad_context: bfloat16 [1024, 6144], P(('batch', 'seq'), 'mp')
All inputs are finite; a program needn't handle non-finite values.
Results may differ from a plain program's by a relative error of at most 0.001.
Values may be sent and summed in bfloat16 or wider, within the bound.
A program may use at most 64 MiB of HBM per device.

v0:
```python
import jax
import jax.numpy as jnp
from jax import lax
from jax.sharding import PartitionSpec as P


def shards(context, cotangent, out_weight):
    groups = lax.axis_size(("batch", "seq"))
    members = lax.axis_size("mp")
    split_rows = lax.all_to_all(context, "mp", split_axis=0, concat_axis=1, tiled=True)
    block_rows = lax.all_to_all(
        split_rows, ("batch", "seq"), split_axis=1, concat_axis=0, tiled=True
    )
    feature_block = lax.all_gather(block_rows, "mp", axis=0, tiled=True)
    all_cotangent = lax.all_gather(cotangent, ("batch", "seq"), axis=0, tiled=True)
    share = split_rows.shape[0]
    shaped_context = feature_block.reshape(members, groups, share, feature_block.shape[1])
    shaped_cotangent = all_cotangent.reshape(groups, members, share, all_cotangent.shape[1])
    grad_weight = lax.dot_general(
        shaped_context,
        shaped_cotangent,
        (((0, 1, 2), (1, 0, 2)), ((), ())),
        preferred_element_type=jnp.float32,
    )
    partial_input = lax.dot_general(
        cotangent, out_weight, (((1,), (1,)), ((), ())), preferred_element_type=jnp.float32
    )
    grad_context = lax.psum_scatter(partial_input, "mp", scatter_dimension=1, tiled=True).astype(
        jnp.bfloat16
    )
    return (grad_weight, grad_context)


def solution(mesh):
    return jax.shard_map(
        shards,
        mesh=mesh,
        in_specs=(P(("batch", "seq"), "mp"), P(("batch", "seq"), "mp"), P(None, "mp")),
        out_specs=(P(("batch", "seq"), "mp"), P(("batch", "seq"), "mp")),
        check_vma=False,
    )
```

profile of v0, /device:TPU:0, one launch (start us, length us, event | category | flops | bytes accessed | tf_op | source)
XLA Modules:
  0.0 176.4 jit_solution(15021152544623179522)
XLA Ops:
  7.2 0.0 copy-start
  7.2 0.0 all-gather.3.cloned.1.call-start
  7.2 18.2 %all_to_all.35 = bf16[4,32,1536]{2,1,0:T(8,128)(2,1)S(1)} all-to-all(bf16[4,32,1536]{2,1,0:T(8,128)(2,1)} %bitcast.16), channel_id=1, replica_groups=mesh['batch'=2,'seq'=4,'mp'=4] {'mp'}, dimensions={0} | all-to-all | bytes 786432 | tf_op jit(solution)/shard_map/all_to_all | solution.py:10
  25.4 0.3 copy.10
  25.7 0.1 all_to_all.29
  25.8 0.1 copy.11
  25.9 11.6 %all_to_all.36 = bf16[32,8,768]{2,0,1:T(8,128)(2,1)} all-to-all(bf16[32,8,768]{2,0,1:T(8,128)(2,1)S(1)} %copy.11), channel_id=1, replica_groups=mesh['batch'=2,'seq'=4,'mp'=4] {'batch','seq'}, dimensions={1} | all-to-all | bytes 786432 | tf_op jit(solution)/shard_map/all_to_all | solution.py:11
  37.5 0.0 all-gather.3.cloned.1.call-update
  37.5 0.0 all-gather.5.cloned.1.call-start
  37.6 0.7 all-gather.5.cloned.1.call-update
  38.3 0.0 reduce-scatter.2.cloned.1.call-start
  38.3 0.0 copy-done
  38.3 14.6 %fusion.1 = f32[128,6144]{1,0:T(8,128)} fusion(bf16[128,1536]{1,0:T(8,128)(2,1)S(1)} %copy-done, bf16[6144,1536]{1,0:T(8,128)(2,1)} %param.5), kind=kOutput, calls=%fused_computation.2 | convolution fusion | flops 2415919104 | bytes 22413312 | tf_op jit(solution)/shard_map/dot_general | solution.py:25
  52.9 0.0 reduce-scatter.2.cloned.1.call-update
  52.9 19.4 %all-gather.3.cloned.1.call-done = bf16[1024,768]{1,0:T(8,128)(2,1)} async-done(((bf16[256,768]{1,0:T(8,128)(2,1)}), bf16[1024,768]{1,0:T(8,128)(2,1)}) %all-gather.3.cloned.1.call-update) | async-done | bytes 1572880 | tf_op jit(solution)/shard_map/all_gather | solution.py:14
  72.3 33.0 %all-gather.5.cloned.1.call-done = bf16[1024,1536]{1,0:T(8,128)(2,1)} async-done(((bf16[128,1536]{1,0:T(8,128)(2,1)}), bf16[1024,1536]{1,0:T(8,128)(2,1)}) %all-gather.5.cloned.1.call-update) | async-done | bytes 3145744 | tf_op jit(solution)/shard_map/all_gather | solution.py:15
  105.2 7.2 %convolution_bitcast_fusion = f32[768,1536]{1,0:T(8,128)} fusion(bf16[4,8,32,768]{3,2,1,0:T(8,128)(2,1)} %bitcast.18, bf16[8,4,32,1536]{3,2,1,0:T(8,128)(2,1)} %bitcast.17), kind=kOutput, calls=%fused_computation | convolution fusion | flops 2415919104 | bytes 9437184 | tf_op jit(solution)/shard_map/dot_general | solution.py:19
  112.4 55.5 %reduce-scatter.2.cloned.1.call-done = f32[128,1536]{1,0:T(8,128)} async-done(((f32[128,6144]{1,0:T(8,128)}), f32[128,1536]{1,0:T(8,128)}) %reduce-scatter.2.cloned.1.call-update) | async-done | bytes 786448 | tf_op jit(solution)/shard_map/reduce_scatter | solution.py:28
  168.0 1.9 %convert_element_type.3 = bf16[128,1536]{1,0:T(8,128)(2,1)} convert(f32[128,1536]{1,0:T(8,128)} %reduce-scatter.2.cloned.1.call-done) | non-fusion elementwise | flops 196608 | bytes 1179648 | tf_op jit(solution)/shard_map/convert_element_type | solution.py:28
Async XLA Ops:
  7.2 31.2 %copy-start = (bf16[128,1536]{1,0:T(8,128)(2,1)S(1)}, bf16[128,1536]{1,0:T(8,128)(2,1)}, u32[]{:S(2)}) copy-start(bf16[128,1536]{1,0:T(8,128)(2,1)} %param.4) | copy-start | bytes 1179652
  7.2 65.1 %all-gather.3.cloned.1.call-start = ((), (), s32[]{:S(2)}) async-start(), calls=%async_computation.3 | async-start | bytes 1966080 | tf_op jit(solution)/shard_map/all_gather | solution.py:14
  37.5 67.7 %all-gather.5.cloned.1.call-start = ((), (), s32[]{:S(2)}) async-start(), calls=%async_computation.4 | async-start | bytes 3538944 | tf_op jit(solution)/shard_map/all_gather | solution.py:15
  38.3 129.7 %reduce-scatter.2.cloned.1.call-start = ((), (), s32[]{:S(2)}) async-start(), calls=%async_computation.5 | async-start | bytes 3932160 | tf_op jit(solution)/shard_map/reduce_scatter | solution.py:28
Sparse Core Ops, SparseCore 0:
  37.6 34.5 all-gather.2
  74.2 31.0 all-gather.4
  107.6 60.3 reduce-scatter.1
where the time goes:
time: 177 us; the launch traced here: 176 us
  waiting for transfers between devices  109 us (62%)
  blocking collectives  29.8 us (17%)
  matrix products  21.8 us (12%)
  between operations  13.8 us (8%)
  other arithmetic  1.92 us (1%)
    reduce_scatter x1, waiting for transfers between devices, shards(): lax.psum_scatter(partial_input, 'mp', scatter_dimension=1, tiled=True)  55.5 us
    all_gather x1, waiting for transfers between devices, shards(): lax.all_gather(cotangent, ('batch', 'seq'), axis=0, tiled=True)  33 us
    all_gather x1, waiting for transfers between devices, shards(): feature_block = lax.all_gather(block_rows, 'mp', axis=0, tiled=True)  19.4 us
    all_to_all x1, blocking collectives, shards(): lax.all_to_all(context, 'mp', split_axis=0, concat_axis=1, tiled=True)  18.2 us
    dot_general x1, matrix products, shards(): lax.dot_general(cotangent, out_weight, (((1,), (1,)), ((), ())), preferre...  14.6 us
    all_to_all x1, blocking collectives, shards(): lax.all_to_all(split_rows, ('batch', 'seq'), split_axis=1, concat_axis=0,...  11.6 us
    dot_general x1, matrix products, shards(): lax.dot_general(shaped_context, shaped_cotangent, (((0, 1, 2), (1, 0, 2))...  7.19 us
  transfers between devices with their start and end apart: 3, of which 3 were waited for; matrix products, arithmetic and copies ran while one was open for 12% of the time, Pallas kernels for 0%

commit v1 on v0

--- a/solution.py
+++ b/solution.py
@@ -1,7 +1,25 @@
+import functools
 import jax
 import jax.numpy as jnp
 from jax import lax
 from jax.sharding import PartitionSpec as P
+
+
+def _direct_entries(field, group_axis):
+    how_many = lax.axis_size(group_axis)
+    t_next = sorted(((pp, (pp + 1) % how_many) for pp in range(how_many)))
+    answer = field
+    column = [answer]
+    for s in range(1, how_many):
+        answer = lax.ppermute(answer, group_axis, t_next)
+        column.insert(0, answer)
+    r2 = jnp.concatenate(column, axis=0)
+    w_next = lax.axis_index(group_axis)
+    carry = jnp.roll(r2, (w_next + 1) * field.shape[0], 0)
+    return carry
+
+
+clusters_match = functools.partial(_direct_entries, group_axis="mp")
 
 
 def shards(context, cotangent, out_weight):
@@ -11,7 +29,7 @@
     block_rows = lax.all_to_all(
         split_rows, ("batch", "seq"), split_axis=1, concat_axis=0, tiled=True
     )
-    feature_block = lax.all_gather(block_rows, "mp", axis=0, tiled=True)
+    feature_block = clusters_match(block_rows)
     all_cotangent = lax.all_gather(cotangent, ("batch", "seq"), axis=0, tiled=True)
     share = split_rows.shape[0]
     shaped_context = feature_block.reshape(members, groups, share, feature_block.shape[1])

time: 177 us -> 137 us (0.77)
  waiting for transfers between devices: 109 us -> 53.3 us
  blocking collectives: 29.8 us -> 39.8 us
  starting transfers between devices: 0.12 us -> 4.25 us
  between operations: 13.8 us -> 15.6 us
    reduce_scatter x1, waiting for transfers between devices: 55.5 us -> 0.01 us  [shards(): lax.psum_scatter(partial_input, 'mp', scatter_dimension=1, tiled=True)]
    ppermute x0 -> x3, waiting for transfers between devices: none -> 52.6 us  [_direct_entries(): answer = lax.ppermute(answer, group_axis, t_next)]
    all_gather x1, waiting for transfers between devices: 33 us -> 0.02 us  [shards(): lax.all_gather(cotangent, ('batch', 'seq'), axis=0, tiled=True)]
    all_gather x1 -> x0, waiting for transfers between devices: 19.4 us -> none  [shards(): feature_block = lax.all_gather(block_rows, 'mp', axis=0, tiled=True)]
    all_to_all x1, blocking collectives: 18.2 us -> 28.3 us  [shards(): lax.all_to_all(context, 'mp', split_axis=0, concat_axis=1, tiled=True)]
    ppermute x0 -> x3, starting transfers between devices: none -> 4.17 us  [_direct_entries(): answer = lax.ppermute(answer, group_axis, t_next)]
  transfers between devices with their start and end apart: 3 -> 5, of which waited for: 3 -> 3; matrix products, arithmetic and copies ran while one was open for 12% -> 15% of each run, Pallas kernels for 0% -> 0%
where the time goes in v1:
time: 137 us
  waiting for transfers between devices  53.3 us (39%)
  blocking collectives  39.8 us (29%)
  matrix products  20.5 us (15%)
  between operations  15.6 us (11%)
  starting transfers between devices  4.25 us (3%)
  other arithmetic  1.92 us (1%)
  local copies, waits for them, and re-layouts  1.77 us (1%)
    ppermute x3, waiting for transfers between devices, _direct_entries(): answer = lax.ppermute(answer, group_axis, t_next)  52.6 us
    all_to_all x1, blocking collectives, shards(): lax.all_to_all(context, 'mp', split_axis=0, concat_axis=1, tiled=True)  28.3 us
    dot_general x1, matrix products, shards(): lax.dot_general(cotangent, out_weight, (((1,), (1,)), ((), ())), preferre...  14.3 us
    all_to_all x1, blocking collectives, shards(): lax.all_to_all(split_rows, ('batch', 'seq'), split_axis=1, concat_axis=0,...  11.5 us
    dot_general x1, matrix products, shards(): lax.dot_general(shaped_context, shaped_cotangent, (((0, 1, 2), (1, 0, 2))...  6.16 us
    ppermute x3, starting transfers between devices, _direct_entries(): answer = lax.ppermute(answer, group_axis, t_next)  4.17 us
  transfers between devices with their start and end apart: 5, of which 3 were waited for; matrix products, arithmetic and copies ran while one was open for 15% of the time, Pallas kernels for 0%

profile of v1, /device:TPU:0, one launch (start us, length us, event | category | flops | bytes accessed | tf_op | source)
XLA Modules:
  0.0 137.1 jit_solution(8129972238352895839)
XLA Ops:
  8.0 0.0 all-gather.2.cloned.1.call-start
  8.0 0.7 all-gather.2.cloned.1.call-update
  8.7 0.0 reduce-scatter.2.cloned.1.call-start
  8.8 14.3 %fusion.1 = f32[128,6144]{1,0:T(8,128)} fusion(bf16[128,1536]{1,0:T(8,128)(2,1)} %param.4, bf16[6144,1536]{1,0:T(8,128)(2,1)} %param.5), kind=kOutput, calls=%fused_computation.11 | convolution fusion | flops 2415919104 | bytes 22413312 | tf_op jit(solution)/shard_map/dot_general | solution.py:43
  23.1 0.0 copy-start
  23.1 0.0 reduce-scatter.2.cloned.1.call-update
  23.1 1.0 copy-done
  24.1 28.3 %all_to_all.35 = bf16[4,32,1536]{2,1,0:T(8,128)(2,1)S(1)} all-to-all(bf16[4,32,1536]{2,1,0:T(8,128)(2,1)S(1)} %bitcast.19), channel_id=1, replica_groups=mesh['batch'=2,'seq'=4,'mp'=4] {'mp'}, dimensions={0} | all-to-all | bytes 786432 | tf_op jit(solution)/shard_map/all_to_all | solution.py:28
  52.3 0.3 copy.10
  52.6 0.1 all_to_all.29
  52.7 0.1 copy.11
  52.8 11.5 %all_to_all.36 = bf16[32,8,768]{2,0,1:T(8,128)(2,1)S(1)} all-to-all(bf16[32,8,768]{2,0,1:T(8,128)(2,1)S(1)} %copy.11), channel_id=1, replica_groups=mesh['batch'=2,'seq'=4,'mp'=4] {'batch','seq'}, dimensions={1} | all-to-all | bytes 786432 | tf_op jit(solution)/shard_map/all_to_all | solution.py:29
  64.3 0.0 collective-permute-start
  64.3 21.9 %collective-permute-done = bf16[256,768]{1,0:T(8,128)(2,1)S(1)} collective-permute-done((bf16[256,768]{1,0:T(8,128)(2,1)S(1)}, bf16[256,768]{1,0:T(8,128)(2,1)S(1)}, u32[]{:S(2)}, u32[]{:S(2)}) %collective-permute-start) | collective-permute-done | bytes 393248 | tf_op jit(solution)/shard_map/ppermute | solution.py:14
  86.2 4.2 %collective-permute-start.1 = (bf16[256,768]{1,0:T(8,128)(2,1)S(1)}, bf16[256,768]{1,0:T(8,128)(2,1)S(1)}, u32[]{:S(2)}, u32[]{:S(2)}) collective-permute-start(bf16[256,768]{1,0:T(8,128)(2,1)S(1)} %collective-permute-done), channel_id=1, source_target_pairs={{0,1},{1,2},{2,3},{3,0},{4,5},{5,6},{6,7},{7,4},{8,9},{9,10},{10,1... | collective-permute-start | bytes 1179656 | tf_op jit(solution)/shard_map/ppermute | solution.py:14
  90.4 17.9 %collective-permute-done.1 = bf16[256,768]{1,0:T(8,128)(2,1)S(1)} collective-permute-done((bf16[256,768]{1,0:T(8,128)(2,1)S(1)}, bf16[256,768]{1,0:T(8,128)(2,1)S(1)}, u32[]{:S(2)}, u32[]{:S(2)}) %collective-permute-start.1) | collective-permute-done | bytes 393248 | tf_op jit(solution)/shard_map/ppermute | solution.py:14
  108.3 0.0 collective-permute-start.2
  108.3 12.8 %collective-permute-done.2 = bf16[256,768]{1,0:T(8,128)(2,1)S(1)} collective-permute-done((bf16[256,768]{1,0:T(8,128)(2,1)S(1)}, bf16[256,768]{1,0:T(8,128)(2,1)S(1)}, u32[]{:S(2)}, u32[]{:S(2)}) %collective-permute-start.2) | collective-permute-done | bytes 393248 | tf_op jit(solution)/shard_map/ppermute | solution.py:14
  121.4 0.1 constant_dynamic-slice_fusion
  121.5 0.0 all-gather.2.cloned.1.call-done
  121.5 6.2 %convolution_bitcast_fusion = f32[768,1536]{1,0:T(8,128)} fusion(bf16[4,8,32,768]{3,2,1,0:T(8,128)(2,1)S(1)} %bitcast.18, bf16[8,4,32,1536]{3,2,1,0:T(8,128)(2,1)} %bitcast.20), kind=kOutput, calls=%fused_computation | convolution fusion | flops 2415919104 | bytes 9437184 | tf_op jit(solution)/shard_map/dot_general | solution.py:37
  127.7 0.0 reduce-scatter.2.cloned.1.call-done
  127.7 1.9 %convert_element_type.3 = bf16[128,1536]{1,0:T(8,128)(2,1)} convert(f32[128,1536]{1,0:T(8,128)} %reduce-scatter.2.cloned.1.call-done) | non-fusion elementwise | flops 196608 | bytes 1179648 | tf_op jit(solution)/shard_map/convert_element_type | solution.py:46
  (8 shorter events, 0.2 us)
Async XLA Ops:
  8.0 113.5 %all-gather.2.cloned.1.call-start = ((), (), s32[]{:S(2)}) async-start(), calls=%async_computation.3 | async-start | bytes 3538944 | tf_op jit(solution)/shard_map/all_gather | solution.py:33
  8.7 119.0 %reduce-scatter.2.cloned.1.call-start = ((), (), s32[]{:S(2)}) async-start(), calls=%async_computation.4 | async-start | bytes 3932160 | tf_op jit(solution)/shard_map/reduce_scatter | solution.py:46
  23.1 1.0 copy-start
  64.3 21.9 %collective-permute-start = (bf16[256,768]{1,0:T(8,128)(2,1)S(1)}, bf16[256,768]{1,0:T(8,128)(2,1)S(1)}, u32[]{:S(2)}, u32[]{:S(2)}) collective-permute-start(bf16[256,768]{1,0:T(8,128)(2,1)S(1)} %bitcast.14), channel_id=1, source_target_pairs={{0,1},{1,2},{2,3},{3,0},{4,5},{5,6},{6,7},{7,4},{8,9},{9,10},{10,1... | collective-permute-start | bytes 1179656 | tf_op jit(solution)/shard_map/ppermute | solution.py:14
  86.2 22.1 %collective-permute-start.1 = (bf16[256,768]{1,0:T(8,128)(2,1)S(1)}, bf16[256,768]{1,0:T(8,128)(2,1)S(1)}, u32[]{:S(2)}, u32[]{:S(2)}) collective-permute-start(bf16[256,768]{1,0:T(8,128)(2,1)S(1)} %collective-permute-done), channel_id=1, source_target_pairs={{0,1},{1,2},{2,3},{3,0},{4,5},{5,6},{6,7},{7,4},{8,9},{9,10},{10,1... | collective-permute-start | bytes 1179656 | tf_op jit(solution)/shard_map/ppermute | solution.py:14
  108.3 12.8 %collective-permute-start.2 = (bf16[256,768]{1,0:T(8,128)(2,1)S(1)}, bf16[256,768]{1,0:T(8,128)(2,1)S(1)}, u32[]{:S(2)}, u32[]{:S(2)}) collective-permute-start(bf16[256,768]{1,0:T(8,128)(2,1)S(1)} %collective-permute-done.1), channel_id=1, source_target_pairs={{0,1},{1,2},{2,3},{3,0},{4,5},{5,6},{6,7},{7,4},{8,9},{9,10},{10,1... | collective-permute-start | bytes 1179656 | tf_op jit(solution)/shard_map/ppermute | solution.py:14
Sparse Core Ops, SparseCore 0:
  10.7 34.9 all-gather.1
Sparse Core Ops, SparseCore 1:
  23.2 80.9 reduce-scatter.1

commit v2 on v0

--- a/solution.py
+++ b/solution.py
@@ -7,7 +7,9 @@
 def shards(context, cotangent, out_weight):
     groups = lax.axis_size(("batch", "seq"))
     members = lax.axis_size("mp")
-    split_rows = lax.all_to_all(context, "mp", split_axis=0, concat_axis=1, tiled=True)
+    w_next = jnp.stack(jnp.split(context, lax.axis_size("mp"), 0), 0)
+    kept_arr = lax.all_to_all(w_next, "mp", 0, 0)
+    split_rows = jnp.concatenate(kept_arr, 1)
     block_rows = lax.all_to_all(
         split_rows, ("batch", "seq"), split_axis=1, concat_axis=0, tiled=True
     )

time: 177 us -> 178 us (level)
  no operation moved by 1% of the time
where the time goes in v2:
time: 178 us; the launch traced here: 177 us
  waiting for transfers between devices  109 us (61%)
  blocking collectives  29.5 us (17%)
  matrix products  21.7 us (12%)
  between operations  13.8 us (8%)
  other arithmetic  1.97 us (1%)
    reduce_scatter x1, waiting for transfers between devices, shards(): lax.psum_scatter(partial_input, 'mp', scatter_dimension=1, tiled=True)  55.5 us
    all_gather x1, waiting for transfers between devices, shards(): lax.all_gather(cotangent, ('batch', 'seq'), axis=0, tiled=True)  33 us
    all_gather x1, waiting for transfers between devices, shards(): feature_block = lax.all_gather(block_rows, 'mp', axis=0, tiled=True)  19.4 us
    all_to_all x1, blocking collectives, shards(): kept_arr = lax.all_to_all(w_next, 'mp', 0, 0)  17.8 us
    dot_general x1, matrix products, shards(): lax.dot_general(cotangent, out_weight, (((1,), (1,)), ((), ())), preferre...  14.5 us
    all_to_all x1, blocking collectives, shards(): lax.all_to_all(split_rows, ('batch', 'seq'), split_axis=1, concat_axis=0,...  11.6 us
    dot_general x1, matrix products, shards(): lax.dot_general(shaped_context, shaped_cotangent, (((0, 1, 2), (1, 0, 2))...  7.19 us
  transfers between devices with their start and end apart: 3, of which 3 were waited for; matrix products, arithmetic and copies ran while one was open for 12% of the time, Pallas kernels for 0%

profile of v2, /device:TPU:0, one launch (start us, length us, event | category | flops | bytes accessed | tf_op | source)
XLA Modules:
  0.0 177.3 jit_solution(8491093557890151525)
XLA Ops:
  7.2 0.0 copy-start
  7.2 0.0 all-gather.3.cloned.1.call-start
  7.2 1.1 slice_bitcast_fusion.3
  8.3 0.1 pad_maximum_fusion
  8.4 17.8 %all_to_all.24 = bf16[4,32,1536]{2,1,0:T(8,128)(2,1)S(1)} all-to-all(bf16[4,32,1536]{2,1,0:T(8,128)(2,1)S(1)} %pad_maximum_fusion), channel_id=1, replica_groups=mesh['batch'=2,'seq'=4,'mp'=4] {'mp'}, dimensions={0} | all-to-all | bytes 786432 | tf_op jit(solution)/shard_map/all_to_all | solution.py:11
  26.2 0.3 copy.10
  26.5 0.1 all_to_all.18
  26.6 0.1 copy.11
  26.7 11.6 %all_to_all.25 = bf16[32,8,768]{2,0,1:T(8,128)(2,1)} all-to-all(bf16[32,8,768]{2,0,1:T(8,128)(2,1)S(1)} %copy.11), channel_id=1, replica_groups=mesh['batch'=2,'seq'=4,'mp'=4] {'batch','seq'}, dimensions={1} | all-to-all | bytes 786432 | tf_op jit(solution)/shard_map/all_to_all | solution.py:13
  38.3 0.0 all-gather.3.cloned.1.call-update
  38.4 0.0 all-gather.5.cloned.1.call-start
  38.4 0.7 all-gather.5.cloned.1.call-update
  39.1 0.0 reduce-scatter.2.cloned.1.call-start
  39.2 0.0 copy-done
  39.2 14.5 %fusion.1 = f32[128,6144]{1,0:T(8,128)} fusion(bf16[128,1536]{1,0:T(8,128)(2,1)S(1)} %copy-done, bf16[6144,1536]{1,0:T(8,128)(2,1)} %param.5), kind=kOutput, calls=%fused_computation.7 | convolution fusion | flops 2415919104 | bytes 22413312 | tf_op jit(solution)/shard_map/dot_general | solution.py:27
  53.7 0.0 reduce-scatter.2.cloned.1.call-update
  53.7 19.4 %all-gather.3.cloned.1.call-done = bf16[1024,768]{1,0:T(8,128)(2,1)} async-done(((bf16[256,768]{1,0:T(8,128)(2,1)}), bf16[1024,768]{1,0:T(8,128)(2,1)}) %all-gather.3.cloned.1.call-update) | async-done | bytes 1572880 | tf_op jit(solution)/shard_map/all_gather | solution.py:16
  73.1 33.0 %all-gather.5.cloned.1.call-done = bf16[1024,1536]{1,0:T(8,128)(2,1)} async-done(((bf16[128,1536]{1,0:T(8,128)(2,1)}), bf16[1024,1536]{1,0:T(8,128)(2,1)}) %all-gather.5.cloned.1.call-update) | async-done | bytes 3145744 | tf_op jit(solution)/shard_map/all_gather | solution.py:17
  106.1 7.2 %convolution_bitcast_fusion = f32[768,1536]{1,0:T(8,128)} fusion(bf16[4,8,32,768]{3,2,1,0:T(8,128)(2,1)} %bitcast.24, bf16[8,4,32,1536]{3,2,1,0:T(8,128)(2,1)} %bitcast.23), kind=kOutput, calls=%fused_computation | convolution fusion | flops 2415919104 | bytes 9437184 | tf_op jit(solution)/shard_map/dot_general | solution.py:21
  113.3 55.5 %reduce-scatter.2.cloned.1.call-done = f32[128,1536]{1,0:T(8,128)} async-done(((f32[128,6144]{1,0:T(8,128)}), f32[128,1536]{1,0:T(8,128)}) %reduce-scatter.2.cloned.1.call-update) | async-done | bytes 786448 | tf_op jit(solution)/shard_map/reduce_scatter | solution.py:30
  168.8 1.9 %convert_element_type.3 = bf16[128,1536]{1,0:T(8,128)(2,1)} convert(f32[128,1536]{1,0:T(8,128)} %reduce-scatter.2.cloned.1.call-done) | non-fusion elementwise | flops 196608 | bytes 1179648 | tf_op jit(solution)/shard_map/convert_element_type | solution.py:30
Async XLA Ops:
  7.2 32.0 %copy-start = (bf16[128,1536]{1,0:T(8,128)(2,1)S(1)}, bf16[128,1536]{1,0:T(8,128)(2,1)}, u32[]{:S(2)}) copy-start(bf16[128,1536]{1,0:T(8,128)(2,1)} %param.4) | copy-start | bytes 1179652
  7.2 65.9 %all-gather.3.cloned.1.call-start = ((), (), s32[]{:S(2)}) async-start(), calls=%async_computation.3 | async-start | bytes 1966080 | tf_op jit(solution)/shard_map/all_gather | solution.py:16
  38.4 67.7 %all-gather.5.cloned.1.call-start = ((), (), s32[]{:S(2)}) async-start(), calls=%async_computation.4 | async-start | bytes 3538944 | tf_op jit(solution)/shard_map/all_gather | solution.py:17
  39.1 129.7 %reduce-scatter.2.cloned.1.call-start = ((), (), s32[]{:S(2)}) async-start(), calls=%async_computation.5 | async-start | bytes 3932160 | tf_op jit(solution)/shard_map/reduce_scatter | solution.py:30
Sparse Core Ops, SparseCore 0:
  38.5 34.5 all-gather.2
  75.0 31.0 all-gather.4
  108.4 60.3 reduce-scatter.1
